TPU v7x, 256 devices: a whole 4x4x8 slice. The times are simulated.
256 devices in a mesh: section: 8 (over z_lo, core), expert: 32 (over y, x, z_hi).
Axes of the slice: x: 4, y: 4, z: 8 (z_hi: 2, z_lo: 4; z = z_hi * 4 + z_lo), core: 2. Of those that a mesh axis runs over, the one named last changes fastest.
Arguments:
- tokens: bfloat16 [8, 4096, 2048], P('section', 'expert'), may hold values from -6 to 6
- routes: int32 [8, 4096, 2], P('section', 'expert'), may hold values from 0 to 15, all different within a row; in each aligned block of 128 rows (0 to 127, 128 to 255, ..., all dimensions but the last counted through in order) at most 32 rows name the same one
- probs: bfloat16 [8, 4096, 2], P('section', 'expert'), may hold values from 0.099609375 to 1
- cotangent: bfloat16 [8, 4096, 2048], P('section', 'expert'), may hold values from -6 to 6
- w_gate: bfloat16 [8, 2048, 12288], P('section', None, 'expert'), may hold values from -0.125 to 0.125
- w_up: bfloat16 [8, 2048, 12288], P('section', None, 'expert'), may hold values from -0.125 to 0.125
- w_down: bfloat16 [8, 12288, 2048], P('section', 'expert'), may hold values from -0.21875 to 0.21875
Outputs:
- upstream: bfloat16 [8, 4096, 2048], P('section', 'expert')
- route_grad: bfloat16 [8, 4096, 2], P('section', 'expert')
- grad_gate: bfloat16 [8, 2048, 12288], P('section', None, 'expert')
- grad_up: bfloat16 [8, 2048, 12288], P('section', None, 'expert')
- grad_down: bfloat16 [8, 12288, 2048], P('section', 'expert')
Inputs may be any that keep to these rules, and one draw needn't show every extreme that they name: `routes`: each token names 2 different experts. In each aligned block of 128 rows (the tokens of one device) no expert is named by more than 32 rows, and in some blocks one expert is named by exactly 32 rows.
All inputs are finite; a program needn't handle non-finite values.
Results may differ from a plain program's by a relative error of at most 0.008.
Values may be sent and summed in bfloat16 or wider, within the bound.
A program may use at most 128 MiB of HBM per device.

v0:
```python
import jax
import jax.numpy as jnp
from jax import lax
from jax.sharding import PartitionSpec as P


def passed_along(block, axis, distance):
    devices = range(lax.axis_size(axis))
    route = [(i - distance, i) for i in devices if i - distance in devices]
    return lax.ppermute(block, axis, route)


def slot_table(route_rows, experts, capacity):
    flat = route_rows.reshape(-1)
    count = flat.shape[0]
    onehot = (flat[:, None] == jnp.arange(experts, dtype=jnp.int32)[None, :]).astype(jnp.int32)
    before = jnp.cumsum(onehot, axis=0, dtype=jnp.int32) - onehot
    position = jnp.sum(before * onehot, axis=1, dtype=jnp.int32)
    slot = flat * capacity + position
    owner = (
        jnp.full((experts * capacity,), -1, jnp.int32)
        .at[slot]
        .set(jnp.arange(count, dtype=jnp.int32))
    )
    return (slot, owner)


def body(tokens, routes, probs, cotangent, w_gate, w_up, w_down):
    units = lax.axis_size("expert")
    experts = units // 2
    tok_rows = tokens.shape[1]
    top_count = routes.shape[2]
    width = tokens.shape[2]
    capacity = 2 * tok_rows * top_count // experts
    slot, owner = slot_table(routes[0], experts, capacity)
    valid = owner >= 0
    entry = jnp.maximum(owner, 0)
    token_of = entry // top_count
    zero_half = jnp.zeros((), jnp.bfloat16)
    send_x = jnp.where(valid[:, None], tokens[0][token_of], zero_half)
    send_dy = jnp.where(valid[:, None], cotangent[0][token_of], zero_half)
    send_p = jnp.where(valid, probs[0].reshape(-1)[entry], zero_half)
    box_x = jnp.broadcast_to(
        send_x.reshape(experts, 1, capacity, width), (experts, 2, capacity, width)
    ).reshape(units, capacity, width)
    box_dy = jnp.broadcast_to(
        send_dy.reshape(experts, 1, capacity, width), (experts, 2, capacity, width)
    ).reshape(units, capacity, width)
    box_p = jnp.broadcast_to(send_p.reshape(experts, 1, capacity), (experts, 2, capacity)).reshape(
        units, capacity
    )
    recv_x, recv_dy, recv_p = (
        lax.all_to_all(box_x, "expert", split_axis=0, concat_axis=0, tiled=True),
        lax.all_to_all(box_dy, "expert", split_axis=0, concat_axis=0, tiled=True),
        lax.all_to_all(box_p, "expert", split_axis=0, concat_axis=0, tiled=True),
    )
    row_count = units * capacity
    xin = recv_x.reshape(row_count, width)
    dyin = recv_dy.reshape(row_count, width)
    pin = recv_p.reshape(row_count).astype(jnp.float32)
    wg = w_gate[0]
    wu = w_up[0]
    wd = w_down[0]
    gate = jnp.dot(xin, wg, preferred_element_type=jnp.float32)
    up_val = jnp.dot(xin, wu, preferred_element_type=jnp.float32)
    sig = jax.nn.sigmoid(gate)
    act = gate * sig
    hidden = (act * up_val).astype(jnp.bfloat16)
    back = lax.dot_general(dyin, wd, (((1,), (1,)), ((), ())), preferred_element_type=jnp.float32)
    route_part = jnp.sum(back * hidden.astype(jnp.float32), axis=1)
    scaled = pin[:, None] * back
    d_gate = (scaled * up_val * sig * (1.0 + gate * (1.0 - sig))).astype(jnp.bfloat16)
    d_up = (scaled * act).astype(jnp.bfloat16)
    weighted = (pin[:, None] * hidden.astype(jnp.float32)).astype(jnp.bfloat16)
    g_gate = lax.dot_general(
        xin, d_gate, (((0,), (0,)), ((), ())), preferred_element_type=jnp.float32
    ).astype(jnp.bfloat16)
    g_up = lax.dot_general(
        xin, d_up, (((0,), (0,)), ((), ())), preferred_element_type=jnp.float32
    ).astype(jnp.bfloat16)
    g_down = lax.dot_general(
        weighted, dyin, (((0,), (0,)), ((), ())), preferred_element_type=jnp.float32
    ).astype(jnp.bfloat16)
    part_dx = lax.dot_general(
        d_gate, wg, (((1,), (1,)), ((), ())), preferred_element_type=jnp.float32
    )
    part_dx = part_dx + lax.dot_general(
        d_up, wu, (((1,), (1,)), ((), ())), preferred_element_type=jnp.float32
    )
    part_dx = part_dx.reshape(units, capacity, width)
    route_part = route_part.reshape(units, capacity)
    got_dx, got_route = (
        lax.all_to_all(part_dx, "expert", split_axis=0, concat_axis=0, tiled=True),
        lax.all_to_all(route_part, "expert", split_axis=0, concat_axis=0, tiled=True),
    )
    total_dx = (
        jnp.sum(got_dx.reshape(experts, 2, capacity, width), axis=1)
        .astype(jnp.bfloat16)
        .reshape(experts * capacity, width)
    )
    total_route = (
        jnp.sum(got_route.reshape(experts, 2, capacity), axis=1)
        .astype(jnp.bfloat16)
        .reshape(experts * capacity)
    )
    layer_dx = (
        total_dx[slot]
        .astype(jnp.float32)
        .reshape(tok_rows, top_count, width)
        .sum(axis=1)
        .astype(jnp.bfloat16)
    )
    route_grad = total_route[slot].reshape(tok_rows, top_count)
    upstream = passed_along(layer_dx[None], "section", -1)
    return (upstream, route_grad[None], g_gate[None], g_up[None], g_down[None])


def solution(mesh):
    in_specs = (
        P("section", "expert", None),
        P("section", "expert", None),
        P("section", "expert", None),
        P("section", "expert", None),
        P("section", None, "expert"),
        P("section", None, "expert"),
        P("section", "expert", None),
    )
    out_specs = (
        P("section", "expert", None),
        P("section", "expert", None),
        P("section", None, "expert"),
        P("section", None, "expert"),
        P("section", "expert", None),
    )
    return jax.shard_map(body, mesh=mesh, in_specs=in_specs, out_specs=out_specs, check_vma=False)
```

profile of v0, /device:TPU:64, one launch (start us, length us, event | category | flops | bytes accessed | tf_op | source)
XLA Modules:
  0.0 528.1 jit_solution(17695429900539420745)
XLA Ops:
  0.7 0.8 broadcast_multiply_fusion
  1.5 0.8 copy.47
  2.3 0.1 eq.29
  2.4 0.1 eq.25
  2.6 0.8 copy.50
  3.3 0.1 reshape_squeeze.4
  3.5 0.1 copy.46
  3.6 0.1 mul.59
  3.8 0.6 reduce-window.6
  4.4 0.2 slice_reduce_fusion
  4.6 0.1 fusion.19
  4.7 1.4 scatter_custom_fusion
  6.1 3.4 gather_fusion
  9.6 0.6 copy.51
  10.2 12.1 %all-to-all-start = ((bf16[32,1,32]{2,1,0:T(2,128)(2,1)}), bf16[32,1,32]{2,1,0:T(2,128)(2,1)S(1)}, u32[]{:S(2)}, u32[]{:S(2)}) async-start(bf16[32,1,32]{2,1,0:T(2,128)(2,1)} %copy.51), calls=%async_computation | async-start | bytes 32768 | tf_op jit(solution)/shard_map/all_to_all | solution.py:55
  22.4 0.1 broadcast_in_dim.72
  22.5 3.3 gather_fusion.2
  25.8 3.3 gather_fusion.1
  29.1 4.6 broadcast_select_fusion.1
  33.7 0.8 all-to-all-done
  34.4 2.1 broadcast_in_dim.77
  36.6 111.0 %all_to_all.33 = bf16[32,32,2048]{2,1,0:T(8,128)(2,1)} all-to-all(bf16[32,32,2048]{2,1,0:T(8,128)(2,1)S(1)} %bitcast.73), channel_id=1, replica_groups=mesh['section'=8,'expert'=32] {'expert'}, dimensions={0} | all-to-all | bytes 8388608 | tf_op jit(solution)/shard_map/all_to_all | solution.py:53
  147.6 2.5 broadcast_in_dim.76
  150.1 5.0 all-to-all-start.1
  155.2 5.3 %fusion.7 = f32[1024,384]{0,1:T(8,128)} fusion(bf16[1024,2048]{1,0:T(8,128)(2,1)} %bitcast.76, bf16[1,2048,384]{2,1,0:T(8,128)(2,1)S(1)} %copy-done), kind=kOutput, calls=%fused_computation.22 | convolution fusion | flops 1610612736 | bytes 7340032 | tf_op jit(solution)/shard_map/dot_general | solution.py:64
  160.6 3.0 fusion.10
  163.5 78.7 %all-to-all-done.1 = bf16[32,32,2048]{2,1,0:T(8,128)(2,1)} async-done(((bf16[32,32,2048]{2,1,0:T(8,128)(2,1)}), bf16[32,32,2048]{2,1,0:T(8,128)(2,1)}, u32[]{:S(2)}, u32[]{:S(2)}) %all-to-all-start.1) | async-done | bytes 4194336 | tf_op jit(solution)/shard_map/all_to_all | solution.py:54
  242.2 6.0 %fusion.3 = (f32[1024]{0:T(1024)S(1)}, bf16[1024,384]{0,1:T(8,128)(2,1)S(1)}, bf16[1024,384]{0,1:T(8,128)(2,1)S(1)}, bf16[1024,384]{0,1:T(8,128)(2,1)S(1)}) fusion(f32[1024,384]{0,1:T(8,128)} %fusion.10, f32[1024,384]{0,1:T(8,128)} %fusion.7, f32[1024]{0:T(1024)S(1)} %reshape.148, bf16[1024,2048]{1,0:T(8,128)(2,1)} %bitcast.7, bf16[1,384,2048]{2,1,0:T(8,128)(2,1)} %param.13), kind=kOutput, calls=%fused_computation.18 | convolution fusion | flops 1618082816 | bytes 11280384 | tf_op jit(solution)/shard_map/dot_general | solution.py:69
  248.2 2.4 fusion.5
  250.7 5.7 %convolution_add_fusion = f32[1024,2048]{1,0:T(8,128)} fusion(f32[1024,2048]{1,0:T(8,128)S(1)} %fusion.5, bf16[1024,384]{0,1:T(8,128)(2,1)S(1)} %get-tuple-element.40, bf16[1,2048,384]{2,1,0:T(8,128)(2,1)S(1)} %copy-done.7), kind=kOutput, calls=%fused_computation.7 | convolution fusion | flops 1612709888 | bytes 19136512 | tf_op jit(solution)/shard_map/dot_general | solution.py:87
  256.3 103.7 %all-to-all-start.3 = ((f32[32,32,2048]{2,1,0:T(8,128)}), f32[32,32,2048]{2,1,0:T(8,128)}, u32[]{:S(2)}, u32[]{:S(2)}) async-start(f32[32,32,2048]{2,1,0:T(8,128)} %bitcast.70), calls=%async_computation.3 | async-start | bytes 16777216 | tf_op jit(solution)/shard_map/all_to_all | solution.py:93
  360.0 5.1 fusion.2
  365.1 109.3 %all-to-all-done.3 = f32[32,32,2048]{2,1,0:T(8,128)} async-done(((f32[32,32,2048]{2,1,0:T(8,128)}), f32[32,32,2048]{2,1,0:T(8,128)}, u32[]{:S(2)}, u32[]{:S(2)}) %all-to-all-start.3) | async-done | bytes 8388640 | tf_op jit(solution)/shard_map/all_to_all | solution.py:93
  474.5 6.2 %bitcast_reduce_fusion = bf16[16,32,2048]{2,1,0:T(8,128)(2,1)} fusion(f32[32,32,2048]{2,1,0:T(8,128)} %all-to-all-done.3), kind=kLoop, calls=%fused_computation.6 | loop fusion | flops 1048576 | bytes 10485760 | tf_op jit(solution)/shard_map/reduce_sum | solution.py:97
  480.7 4.2 gather_fusion.3
  484.9 0.7 convert_element_type.84
  485.7 3.6 reduce
  489.3 1.9 collective-permute-start
  491.2 5.7 %fusion = bf16[1,2048,384]{2,1,0:T(8,128)(2,1)} fusion(bf16[1024,2048]{1,0:T(8,128)(2,1)} %bitcast.77, bf16[1024,384]{0,1:T(8,128)(2,1)S(1)} %copy-done.9), kind=kOutput, calls=%fused_computation.11 | convolution fusion | flops 1611399168 | bytes 6553600 | tf_op jit(solution)/shard_map/dot_general | solution.py:75
  497.0 0.7 all_to_all.26
  497.6 15.1 %all-to-all-start.4 = ((f32[32,1,32]{2,1,0:T(1,128)}), f32[32,1,32]{2,1,0:T(1,128)S(1)}, u32[]{:S(2)}, u32[]{:S(2)}) async-start(f32[32,1,32]{2,1,0:T(1,128)} %all_to_all.26), calls=%async_computation.4 | async-start | bytes 32768 | tf_op jit(solution)/shard_map/all_to_all | solution.py:94
  512.8 5.8 %fusion.1 = bf16[1,2048,384]{2,1,0:T(8,128)(2,1)} fusion(bf16[1024,2048]{1,0:T(8,128)(2,1)} %bitcast.78, bf16[1024,384]{0,1:T(8,128)(2,1)S(1)} %get-tuple-element.40), kind=kOutput, calls=%fused_computation.12 | convolution fusion | flops 1611399168 | bytes 6553600 | tf_op jit(solution)/shard_map/dot_general | solution.py:78
  518.6 5.9 %all-to-all-done.4 = f32[32,1,32]{2,1,0:T(1,128)S(1)} async-done(((f32[32,1,32]{2,1,0:T(1,128)}), f32[32,1,32]{2,1,0:T(1,128)S(1)}, u32[]{:S(2)}, u32[]{:S(2)}) %all-to-all-start.4) | async-done | bytes 4128 | tf_op jit(solution)/shard_map/all_to_all | solution.py:94
  524.6 0.1 convert_element_type.91
  524.6 1.9 gather_fusion.4
  526.6 0.2 broadcast_in_dim_reshape.3
  526.7 0.6 copy.53
  527.3 0.8 copy.58
  (35 shorter events, 0.4 us)
Async XLA Ops:
  0.6 154.6 %copy-start = (bf16[1,2048,384]{2,1,0:T(8,128)(2,1)S(1)}, bf16[1,2048,384]{2,1,0:T(8,128)(2,1)}, u32[]{:S(2)}) copy-start(bf16[1,2048,384]{2,1,0:T(8,128)(2,1)} %param.11) | copy-start | bytes 4718596
  0.6 21.8 %copy-start.2 = (bf16[1,128,2048]{2,1,0:T(8,128)(2,1)S(1)}, bf16[1,128,2048]{2,1,0:T(8,128)(2,1)}, u32[]{:S(2)}) copy-start(bf16[1,128,2048]{2,1,0:T(8,128)(2,1)} %param.7) | copy-start | bytes 1572868
  10.2 24.2 %all-to-all-start = ((bf16[32,1,32]{2,1,0:T(2,128)(2,1)}), bf16[32,1,32]{2,1,0:T(2,128)(2,1)S(1)}, u32[]{:S(2)}, u32[]{:S(2)}) async-start(bf16[32,1,32]{2,1,0:T(2,128)(2,1)} %copy.51), calls=%async_computation | async-start | bytes 32768 | tf_op jit(solution)/shard_map/all_to_all | solution.py:55
  22.5 3.3 copy-start.3
  36.6 111.1 %copy-start.4 = (bf16[16,32,2048]{2,1,0:T(8,128)(2,1)S(1)}, bf16[16,32,2048]{2,1,0:T(8,128)(2,1)}, u32[]{:S(2)}) copy-start(bf16[16,32,2048]{2,1,0:T(8,128)(2,1)} %get-tuple-element.41) | copy-start | bytes 6291460
  150.1 92.1 %all-to-all-start.1 = ((bf16[32,32,2048]{2,1,0:T(8,128)(2,1)}), bf16[32,32,2048]{2,1,0:T(8,128)(2,1)}, u32[]{:S(2)}, u32[]{:S(2)}) async-start(bf16[32,32,2048]{2,1,0:T(8,128)(2,1)} %bitcast.72), calls=%async_computation.1 | async-start | bytes 8388608 | tf_op jit(solution)/shard_map/all_to_all | solution.py:54
  155.2 5.3 %copy-start.5 = (bf16[32,32,2048]{2,1,0:T(8,128)(2,1)S(1)}, bf16[32,32,2048]{2,1,0:T(8,128)(2,1)}, u32[]{:S(2)}) copy-start(bf16[32,32,2048]{2,1,0:T(8,128)(2,1)} %all_to_all.33) | copy-start | bytes 12582916
  155.2 5.3 %copy-start.6 = (bf16[1,2048,384]{2,1,0:T(8,128)(2,1)S(1)}, bf16[1,2048,384]{2,1,0:T(8,128)(2,1)}, u32[]{:S(2)}) copy-start(bf16[1,2048,384]{2,1,0:T(8,128)(2,1)} %param.12) | copy-start | bytes 4718596
  248.2 2.4 copy-start.8
  248.2 2.4 copy-start.7
  256.3 218.2 %all-to-all-start.3 = ((f32[32,32,2048]{2,1,0:T(8,128)}), f32[32,32,2048]{2,1,0:T(8,128)}, u32[]{:S(2)}, u32[]{:S(2)}) async-start(f32[32,32,2048]{2,1,0:T(8,128)} %bitcast.70), calls=%async_computation.3 | async-start | bytes 16777216 | tf_op jit(solution)/shard_map/all_to_all | solution.py:93
  485.6 5.6 %copy-start.9 = (bf16[1024,384]{0,1:T(8,128)(2,1)S(1)}, bf16[1024,384]{0,1:T(8,128)(2,1)}, u32[]{:S(2)}) copy-start(bf16[1024,384]{0,1:T(8,128)(2,1)} %copy-done.8) | copy-start | bytes 2359300
  489.3 38.0 %collective-permute-start = (bf16[1,128,2048]{2,1,0:T(8,128)(2,1)}, bf16[1,128,2048]{2,1,0:T(8,128)(2,1)S(1)}, u32[]{:S(2)}, u32[]{:S(2)}) collective-permute-start(bf16[1,128,2048]{2,1,0:T(8,128)(2,1)} %bitcast.18), channel_id=1, source_target_pairs={{32,0},{64,32},{96,64},{128,96},{160,128},{192,160},{224,192},{33,... | collective-permute-start | bytes 1572872 | tf_op jit(solution)/shard_map/ppermute | solution.py:10
  497.6 26.9 %all-to-all-start.4 = ((f32[32,1,32]{2,1,0:T(1,128)}), f32[32,1,32]{2,1,0:T(1,128)S(1)}, u32[]{:S(2)}, u32[]{:S(2)}) async-start(f32[32,1,32]{2,1,0:T(1,128)} %all_to_all.26), calls=%async_computation.4 | async-start | bytes 32768 | tf_op jit(solution)/shard_map/all_to_all | solution.py:94
  512.8 15.4 %copy-start.1 = (bf16[1,2048,384]{2,1,0:T(8,128)(2,1)S(1)}, bf16[1,2048,384]{2,1,0:T(8,128)(2,1)}, u32[]{:S(2)}) copy-start(bf16[1,2048,384]{2,1,0:T(8,128)(2,1)} %param.11) | copy-start | bytes 4718596
where the time goes:
time: 529 us; the launch traced here: 528 us
  waiting for transfers between devices  195 us (37%)
  starting transfers between devices  138 us (26%)
  blocking collectives  111 us (21%)
  matrix products  39.1 us (7%)
  local copies, waits for them, and re-layouts  28.5 us (5%)
  other arithmetic  16.1 us (3%)
    all_to_all x1, blocking collectives, body(): lax.all_to_all(box_x, 'expert', split_axis=0, concat_axis=0, tiled=True)  111 us
    all_to_all x1, waiting for transfers between devices, body(): lax.all_to_all(part_dx, 'expert', split_axis=0, concat_axis=0, tiled=True)  109 us
    all_to_all x1, starting transfers between devices, body(): lax.all_to_all(part_dx, 'expert', split_axis=0, concat_axis=0, tiled=True)  104 us
    all_to_all x1, waiting for transfers between devices, body(): lax.all_to_all(box_dy, 'expert', split_axis=0, concat_axis=0, tiled=True)  78.7 us
    all_to_all x1, starting transfers between devices, body(): lax.all_to_all(route_part, 'expert', split_axis=0, concat_axis=0, tiled=T...  15.1 us
    all_to_all x1, starting transfers between devices, body(): lax.all_to_all(box_p, 'expert', split_axis=0, concat_axis=0, tiled=True)  12.1 us
  transfers between devices with their start and end apart: 5, of which 4 were waited for; matrix products, arithmetic and copies ran while one was open for 7% of the time, Pallas kernels for 0%

commit v1 on v0

v1 whole, which is shorter than its diff:
```python
import jax
import jax.numpy as jnp
from jax import lax
from jax.experimental import pallas as pl
from jax.experimental.pallas import tpu as pltpu
from jax.sharding import PartitionSpec as P

BF = jnp.bfloat16
F32 = jnp.float32
SIDE = 4
EXPERTS = SIDE * SIDE
SLOTS = 32
TOK = 128
WIDTH = 2048
HALF = 384
TAIL = 128
CHUNK = 8
MESH = pl.DeviceIdType.MESH


def dot(a, b, dims):
    return lax.dot_general(a, b, (dims, ((), ())), preferred_element_type=F32)


def kernel(
    x_ref, routes_ref, probs_ref, dy_ref, wg_ref, wu_ref, wd_ref,
    up_ref, rg_ref, gg_ref, gu_ref, gd_ref,
    wgu, wdn, pair, metas, stage, rows, dab, hid, ret_out, ret_in, ggu, gdn,
    fin_out, fin_in, rfin_out, rfin_in,
    w_sem, z_send, z_recv, d_send, d_recv, r_send, r_recv, f_send, f_recv, l_sem, o_sem,
):
    sec = lax.axis_index("section")
    unit = lax.axis_index("expert")
    n_sec = lax.axis_size("section")
    zh = unit % 2
    ex = (unit // 2) % SIDE
    ey = unit // (2 * SIDE)
    mate = unit + 1 - 2 * zh
    prev = (sec + n_sec - 1) % n_sec

    def ahead(o):
        dx = o % SIDE
        dy = (o + o // SIDE) % SIDE
        return ((ey + dy) % SIDE * SIDE + (ex + dx) % SIDE) * 2 + zh

    def behind(o):
        dx = o % SIDE
        dy = (o + o // SIDE) % SIDE
        return ((ey + SIDE - dy) % SIDE * SIDE + (ex + SIDE - dx) % SIDE) * 2 + zh

    w_copies = [
        pltpu.make_async_copy(wg_ref, wgu.at[:, pl.ds(0, HALF)], w_sem.at[0]),
        pltpu.make_async_copy(wu_ref, wgu.at[:, pl.ds(HALF, HALF)], w_sem.at[1]),
        pltpu.make_async_copy(wd_ref, wdn, w_sem.at[2]),
    ]

    def to_mate(src, dst, i):
        return pltpu.make_async_remote_copy(
            src_ref=src, dst_ref=dst, send_sem=z_send.at[i], recv_sem=z_recv.at[i],
            device_id={"expert": mate}, device_id_type=MESH)

    z_copies = [
        to_mate(x_ref, pair.at[0], 0),
        to_mate(dy_ref, pair.at[1], 1),
        to_mate(metas.at[0], metas.at[1], 2),
    ]

    def dispatch(g, o):
        f = g * EXPERTS + o
        return pltpu.make_async_remote_copy(
            src_ref=stage.at[f], dst_ref=rows.at[f], send_sem=d_send.at[f], recv_sem=d_recv.at[f],
            device_id={"expert": ahead(o)}, device_id_type=MESH)

    def local_dispatch(g):
        f = g * EXPERTS
        return pltpu.make_async_copy(stage.at[f], rows.at[f], l_sem.at[g])

    def giveback(g, o):
        f = g * EXPERTS + o
        return pltpu.make_async_remote_copy(
            src_ref=ret_out.at[f], dst_ref=ret_in.at[f], send_sem=r_send.at[f], recv_sem=r_recv.at[f],
            device_id={"expert": behind(o)}, device_id_type=MESH)

    def local_giveback(g):
        f = g * EXPERTS
        return pltpu.make_async_copy(ret_out.at[f], ret_in.at[f], l_sem.at[g])

    def final(i):
        src, dst = ((fin_out.at[0], fin_in.at[0]), (fin_out.at[1], fin_in.at[1]), (rfin_out, rfin_in))[i]
        to = ({"section": prev}, {"section": prev, "expert": mate}, {"expert": mate})[i]
        return pltpu.make_async_remote_copy(
            src_ref=src, dst_ref=dst, send_sem=f_send.at[i], recv_sem=f_recv.at[i],
            device_id=to, device_id_type=MESH)

    z_copies[0].start()
    z_copies[1].start()
    for c in w_copies:
        c.start()

    lane = lax.broadcasted_iota(jnp.int32, (TOK, TOK), 1)
    row = lax.broadcasted_iota(jnp.int32, (TOK, TOK), 0)
    routes = routes_ref[...]
    probs = probs_ref[...].astype(F32)
    named = [routes[:, k : k + 1] for k in range(2)]
    member = ((named[0] == lane) | (named[1] == lane)).astype(BF)
    before = dot((lane < row).astype(BF), member, ((1,), (0,)))
    meta = jnp.zeros((TOK, TOK), F32)
    for k in range(2):
        place = jnp.sum(jnp.where(lane == named[k], before, 0.0), axis=1, keepdims=True)
        dx = (named[k] + (SIDE - ex)) % SIDE
        dy = (named[k] // SIDE + (SIDE - ey)) % SIDE
        order = dx + SIDE * ((dy + SIDE - dx) % SIDE)
        meta = jnp.where(lane == 2 * k, order.astype(F32), meta)
        meta = jnp.where(lane == 2 * k + 1, place, meta)
        meta = jnp.where(lane == 4 + k, probs[:, k : k + 1], meta)
    metas[0] = meta.astype(BF)
    z_copies[2].start()

    def picks(g):
        m = metas[g].astype(F32)
        slot_of = lax.broadcasted_iota(jnp.int32, (TOK, EXPERTS * SLOTS), 1)
        slots = [(m[:, 2 * k : 2 * k + 1] * SLOTS + m[:, 2 * k + 1 : 2 * k + 2]).astype(jnp.int32) for k in range(2)]
        return [slot_of == s for s in slots], [m[:, 4 + k : 5 + k] for k in range(2)]

    def pack(g, x_in, dy_in):
        hits, ps = picks(g)
        ones = (hits[0] | hits[1]).astype(BF)
        scaled = (jnp.where(hits[0], ps[0], 0.0) + jnp.where(hits[1], ps[1], 0.0)).astype(BF)
        for half in range(EXPERTS // CHUNK):
            cols = slice(half * CHUNK * SLOTS, (half + 1) * CHUNK * SLOTS)
            base = g * EXPERTS + half * CHUNK
            for which, (mat, src) in enumerate(((ones, x_in), (scaled, dy_in))):
                got = dot(mat[:, cols], src[...], ((0,), (0,))).astype(BF)
                stage[pl.ds(base, CHUNK), which] = got.reshape(CHUNK, SLOTS, WIDTH)
            if half == 0:
                local_dispatch(g).start()
            for o in range(half * CHUNK, (half + 1) * CHUNK):
                if o:
                    dispatch(g, o).start()

    pack(0, x_ref, dy_ref)
    for c in w_copies:
        c.wait()

    def work(i, _):
        g = i // (EXPERTS // CHUNK)
        first = (i % (EXPERTS // CHUNK)) * CHUNK

        @pl.when(i == 1)
        def _():
            for c in z_copies:
                c.wait_recv()
            pack(1, pair.at[0], pair.at[1])

        @pl.when(first == 0)
        def _():
            local_dispatch(g).wait()

        def arrive(j, _):
            o = first + j

            @pl.when(o > 0)
            def _():
                dispatch(g, o).wait_recv()

            return 0

        lax.fori_loop(0, CHUNK, arrive, 0)
        f = pl.multiple_of(i * CHUNK, CHUNK)
        r = pl.multiple_of(i * CHUNK * SLOTS, CHUNK * SLOTS)
        n = CHUNK * SLOTS
        x = rows[pl.ds(f, CHUNK), 0].reshape(n, WIDTH)
        dyp = rows[pl.ds(f, CHUNK), 1].reshape(n, WIDTH)
        ab = dot(x, wgu[...], ((1,), (0,)))
        q = dot(dyp, wdn[...], ((1,), (1,)))
        a, b = ab[:, :HALF], ab[:, HALF:]
        sig = jax.nn.sigmoid(a)
        act = a * sig
        h = (act * b).astype(BF)
        part = jnp.sum(q * h.astype(F32), axis=1, keepdims=True)
        d_gate = (q * b * sig * (1.0 + a * (1.0 - sig))).astype(BF)
        d_up = (q * act).astype(BF)
        hid[pl.ds(r, n), :] = h
        dab[pl.ds(r, n), pl.ds(0, HALF)] = d_gate
        dab[pl.ds(r, n), pl.ds(HALF, HALF)] = d_up
        both = dab[pl.ds(r, n), :]
        back = dot(both, wgu[...], ((1,), (1,))).astype(BF)
        ret_out[pl.ds(f, CHUNK), :, pl.ds(0, WIDTH)] = back.reshape(CHUNK, SLOTS, WIDTH)
        high = part.astype(BF).astype(F32)
        at = lax.broadcasted_iota(jnp.int32, (n, TAIL), 1)
        tail = jnp.where(at == 0, high, jnp.where(at == 1, part - high, 0.0)).astype(BF)
        ret_out[pl.ds(f, CHUNK), :, pl.ds(WIDTH, TAIL)] = tail.reshape(CHUNK, SLOTS, TAIL)

        @pl.when(first == 0)
        def _():
            local_giveback(g).start()

        def leave(j, _):
            o = first + j

            @pl.when(o > 0)
            def _():
                giveback(g, o).start()

            return 0

        lax.fori_loop(0, CHUNK, leave, 0)
        return 0

    lax.fori_loop(0, 2 * EXPERTS // CHUNK, work, 0)

    n_rows = 2 * EXPERTS * SLOTS
    tile = 256

    def grads(t, _):
        cols = pl.ds(pl.multiple_of(t * tile, tile), tile)
        xt = rows[:, 0, :, cols].reshape(n_rows, tile)
        ggu[cols, :] = dot(xt, dab[...], ((0,), (0,))).astype(BF)
        dyt = rows[:, 1, :, cols].reshape(n_rows, tile)
        gdn[:, cols] = dot(hid[...], dyt, ((0,), (0,))).astype(BF)
        return 0

    lax.fori_loop(0, WIDTH // tile, grads, 0)
    o_copies = [
        pltpu.make_async_copy(ggu.at[:, pl.ds(0, HALF)], gg_ref, o_sem.at[0]),
        pltpu.make_async_copy(ggu.at[:, pl.ds(HALF, HALF)], gu_ref, o_sem.at[1]),
        pltpu.make_async_copy(gdn, gd_ref, o_sem.at[2]),
    ]
    for c in o_copies:
        c.start()

    def join(g):
        local_giveback(g).wait()

        def arrive(o, _):
            giveback(g, o).wait_recv()
            return 0

        lax.fori_loop(1, EXPERTS, arrive, 0)
        hits, _ = picks(g)
        got = ret_in.at[pl.ds(g * EXPERTS, EXPERTS)]
        mine = (hits[0] | hits[1]).astype(BF)
        dx = dot(mine, got[:, :, pl.ds(0, WIDTH)].reshape(EXPERTS * SLOTS, WIDTH), ((1,), (0,)))
        fin_out[g] = dx.astype(BF)
        final(g).start()
        tail = got[:, :, pl.ds(WIDTH, TAIL)].reshape(EXPERTS * SLOTS, TAIL)
        parts = [dot(hits[k].astype(BF), tail, ((1,), (0,))) for k in range(2)]
        return [v[:, 0:1] + v[:, 1:2] for v in parts]

    own = join(0)
    other = join(1)
    rfin_out[...] = jnp.where(lane == 0, other[0], jnp.where(lane == 1, other[1], 0.0))
    final(2).start()

    final(2).wait_recv()
    there = rfin_in[...]
    total = [(own[k] + there[:, k : k + 1]) / probs[:, k : k + 1] for k in range(2)]
    pairs = jnp.where(lane == 0, total[0], jnp.where(lane == 1, total[1], 0.0))
    rg_ref[...] = pairs[:, :2].astype(BF)
    final(0).wait_recv()
    final(1).wait_recv()
    summed = fin_in[0].astype(F32) + fin_in[1].astype(F32)
    up_ref[...] = jnp.where(sec == n_sec - 1, 0.0, summed).astype(BF)

    for c in z_copies:
        c.wait_send()
    for i in range(3):
        final(i).wait_send()

    def left(o, _):
        for g in range(2):
            dispatch(g, o).wait_send()
            giveback(g, o).wait_send()
        return 0

    lax.fori_loop(1, EXPERTS, left, 0)
    for c in o_copies:
        c.wait()


def body(tokens, routes, probs, cotangent, w_gate, w_up, w_down):
    vmem = pl.BlockSpec(memory_space=pltpu.VMEM)
    hbm = pl.BlockSpec(memory_space=pl.ANY)
    blocks = 2 * EXPERTS
    n_rows = blocks * SLOTS
    out = pl.pallas_call(
        kernel,
        out_shape=(
            jax.ShapeDtypeStruct((TOK, WIDTH), BF),
            jax.ShapeDtypeStruct((TOK, 2), BF),
            jax.ShapeDtypeStruct((WIDTH, HALF), BF),
            jax.ShapeDtypeStruct((WIDTH, HALF), BF),
            jax.ShapeDtypeStruct((HALF, WIDTH), BF),
        ),
        in_specs=[vmem, vmem, vmem, vmem, hbm, hbm, hbm],
        out_specs=(vmem, vmem, hbm, hbm, hbm),
        scratch_shapes=[
            pltpu.VMEM((WIDTH, 2 * HALF), BF),
            pltpu.VMEM((HALF, WIDTH), BF),
            pltpu.VMEM((2, TOK, WIDTH), BF),
            pltpu.VMEM((2, TOK, TOK), BF),
            pltpu.VMEM((blocks, 2, SLOTS, WIDTH), BF),
            pltpu.VMEM((blocks, 2, SLOTS, WIDTH), BF),
            pltpu.VMEM((n_rows, 2 * HALF), BF),
            pltpu.VMEM((n_rows, HALF), BF),
            pltpu.VMEM((blocks, SLOTS, WIDTH + TAIL), BF),
            pltpu.VMEM((blocks, SLOTS, WIDTH + TAIL), BF),
            pltpu.VMEM((WIDTH, 2 * HALF), BF),
            pltpu.VMEM((HALF, WIDTH), BF),
            pltpu.VMEM((2, TOK, WIDTH), BF),
            pltpu.VMEM((2, TOK, WIDTH), BF),
            pltpu.VMEM((TOK, TOK), F32),
            pltpu.VMEM((TOK, TOK), F32),
            pltpu.SemaphoreType.DMA((3,)),
            pltpu.SemaphoreType.DMA((3,)),
            pltpu.SemaphoreType.DMA((3,)),
            pltpu.SemaphoreType.DMA((blocks,)),
            pltpu.SemaphoreType.DMA((blocks,)),
            pltpu.SemaphoreType.DMA((blocks,)),
            pltpu.SemaphoreType.DMA((blocks,)),
            pltpu.SemaphoreType.DMA((3,)),
            pltpu.SemaphoreType.DMA((3,)),
            pltpu.SemaphoreType.DMA((2,)),
            pltpu.SemaphoreType.DMA((3,)),
        ],
        compiler_params=pltpu.CompilerParams(has_side_effects=True, vmem_limit_bytes=58 << 20),
        name="expert_backward",
    )(tokens[0], routes[0], probs[0], cotangent[0], w_gate[0], w_up[0], w_down[0])
    return tuple(o[None] for o in out)


def solution(mesh):
    by_token = P("section", "expert", None)
    by_column = P("section", None, "expert")
    return jax.shard_map(
        body,
        mesh=mesh,
        in_specs=(by_token, by_token, by_token, by_token, by_column, by_column, by_token),
        out_specs=(by_token, by_token, by_column, by_column, by_token),
        check_vma=False,
    )
```

time: 529 us -> 258 us (0.49)
  the two profiles are of different devices: /device:TPU:64 before, /device:TPU:27 now
where the time goes in v1:
time: 258 us
  Pallas kernels  245 us (95%)
  local copies, waits for them, and re-layouts  12 us (5%)
    pallas_call x1, Pallas kernels, body(): pl.pallas_call(kernel, out_shape=(jax.ShapeDtypeStruct((TOK, WIDTH), BF),...  245 us
    unnamed x11, local copies, waits for them, and re-layouts  12 us

profile of v1, /device:TPU:27, one launch (start us, length us, event | category | flops | bytes accessed | tf_op | source)
XLA Modules:
  0.0 257.7 jit_solution(5835903676621106210)
XLA Ops:
  0.6 1.4 copy.13
  2.0 1.4 copy.12
  3.4 245.1 %expert_backward.1 = (bf16[128,2048]{1,0:T(8,128)(2,1)}, bf16[128,2]{1,0:T(8,128)(2,1)}, bf16[2048,384]{1,0:T(8,128)(2,1)}, bf16[2048,384]{1,0:T(8,128)(2,1)}, bf16[384,2048]{1,0:T(8,128)(2,1)}) custom-call(bf16[128,2048]{1,0:T(8,128)(2,1)} %bitcast.18, s32[128,2]{1,0:T(8,128)} %bitcast.21, bf16[128,2]{1,0:T(8,128)(2,1)} %bitcast.22, ...), custom_call_target="tpu_custom_call" | custom-call | tf_op jit(solution)/shard_map/expert_backward/pallas_call | solution.py:286
  248.6 1.4 copy.14
  249.9 1.9 copy.19
  251.8 0.0 copy-start.1
  251.8 2.8 %copy.20 = bf16[1,2048,384]{2,1,0:T(8,128)(2,1)} copy(bf16[1,2048,384]{2,1,0:T(8,128)(2,1)} %bitcast.14) | data formatting | bytes 3145728
  254.6 0.0 copy-done.1
  254.6 0.0 copy-start
  254.6 1.1 copy.21
  255.8 0.8 copy-done
  256.6 1.1 copy.22
Async XLA Ops:
  251.8 2.8 %copy-start.1 = (bf16[2048,384]{1,0:T(8,128)(2,1)S(1)}, bf16[2048,384]{1,0:T(8,128)(2,1)}, u32[]{:S(2)}) copy-start(bf16[2048,384]{1,0:T(8,128)(2,1)} %get-tuple-element.13) | copy-start | bytes 4718596
  254.6 2.0 copy-start

commit v2 on v1

--- a/solution.py
+++ b/solution.py
@@ -15,6 +15,9 @@
 HALF = 384
 TAIL = 128
 CHUNK = 8
+REST = 512
+MAIN = WIDTH - REST
+EARLY = 12
 MESH = pl.DeviceIdType.MESH
 
 
@@ -25,9 +28,9 @@
 def kernel(
     x_ref, routes_ref, probs_ref, dy_ref, wg_ref, wu_ref, wd_ref,
     up_ref, rg_ref, gg_ref, gu_ref, gd_ref,
-    wgu, wdn, pair, metas, stage, rows, dab, hid, ret_out, ret_in, ggu, gdn,
+    wgu, wdn, pair, metas, stage, stage_b, rows, rows_b, dab, hid, ret_out, ret_in, ggu, gdn,
     fin_out, fin_in, rfin_out, rfin_in,
-    w_sem, z_send, z_recv, d_send, d_recv, r_send, r_recv, f_send, f_recv, l_sem, o_sem,
+    w_sem, z_send, z_recv, d_send, d_recv, b_send, b_recv, c_send, c_recv, r_send, r_recv, f_send, f_recv, l_sem, o_sem,
 ):
     sec = lax.axis_index("section")
     unit = lax.axis_index("expert")
@@ -60,8 +63,8 @@
             device_id={"expert": mate}, device_id_type=MESH)
 
     z_copies = [
-        to_mate(x_ref, pair.at[0], 0),
-        to_mate(dy_ref, pair.at[1], 1),
+        to_mate(x_ref.at[:, pl.ds(0, MAIN)], pair.at[0], 0),
+        to_mate(dy_ref.at[:, pl.ds(0, MAIN)], pair.at[1], 1),
         to_mate(metas.at[0], metas.at[1], 2),
     ]
 
@@ -71,9 +74,15 @@
             src_ref=stage.at[f], dst_ref=rows.at[f], send_sem=d_send.at[f], recv_sem=d_recv.at[f],
             device_id={"expert": ahead(o)}, device_id_type=MESH)
 
-    def local_dispatch(g):
-        f = g * EXPERTS
-        return pltpu.make_async_copy(stage.at[f], rows.at[f], l_sem.at[g])
+    def dispatch_rest(o):
+        return pltpu.make_async_remote_copy(
+            src_ref=stage_b.at[o], dst_ref=rows_b.at[o], send_sem=b_send.at[o], recv_sem=b_recv.at[o],
+            device_id={"expert": ahead(o)}, device_id_type=MESH)
+
+    def across(o):
+        return pltpu.make_async_remote_copy(
+            src_ref=rows_b.at[o], dst_ref=rows_b.at[EXPERTS + o], send_sem=c_send.at[o], recv_sem=c_recv.at[o],
+            device_id={"expert": mate}, device_id_type=MESH)
 
     def giveback(g, o):
         f = g * EXPERTS + o
@@ -99,9 +108,15 @@
 
     lane = lax.broadcasted_iota(jnp.int32, (TOK, TOK), 1)
     row = lax.broadcasted_iota(jnp.int32, (TOK, TOK), 0)
-    routes = routes_ref[...]
-    probs = probs_ref[...].astype(F32)
-    named = [routes[:, k : k + 1] for k in range(2)]
+    diagonal = row == lane
+
+    def column(v):
+        return jnp.sum(jnp.where(diagonal, v, 0.0), axis=1, keepdims=True)
+
+    routes = routes_ref[...].astype(F32)
+    chances = probs_ref[...].astype(F32)
+    named = [column(routes[k : k + 1, :]).astype(jnp.int32) for k in range(2)]
+    probs = [column(chances[k : k + 1, :]) for k in range(2)]
     member = ((named[0] == lane) | (named[1] == lane)).astype(BF)
     before = dot((lane < row).astype(BF), member, ((1,), (0,)))
     meta = jnp.zeros((TOK, TOK), F32)
@@ -112,7 +127,7 @@
         order = dx + SIDE * ((dy + SIDE - dx) % SIDE)
         meta = jnp.where(lane == 2 * k, order.astype(F32), meta)
         meta = jnp.where(lane == 2 * k + 1, place, meta)
-        meta = jnp.where(lane == 4 + k, probs[:, k : k + 1], meta)
+        meta = jnp.where(lane == 4 + k, probs[k], meta)
     metas[0] = meta.astype(BF)
     z_copies[2].start()
 
@@ -122,39 +137,57 @@
         slots = [(m[:, 2 * k : 2 * k + 1] * SLOTS + m[:, 2 * k + 1 : 2 * k + 2]).astype(jnp.int32) for k in range(2)]
         return [slot_of == s for s in slots], [m[:, 4 + k : 5 + k] for k in range(2)]
 
-    def pack(g, x_in, dy_in):
+    def masks(g):
         hits, ps = picks(g)
         ones = (hits[0] | hits[1]).astype(BF)
         scaled = (jnp.where(hits[0], ps[0], 0.0) + jnp.where(hits[1], ps[1], 0.0)).astype(BF)
-        for half in range(EXPERTS // CHUNK):
-            cols = slice(half * CHUNK * SLOTS, (half + 1) * CHUNK * SLOTS)
-            base = g * EXPERTS + half * CHUNK
-            for which, (mat, src) in enumerate(((ones, x_in), (scaled, dy_in))):
-                got = dot(mat[:, cols], src[...], ((0,), (0,))).astype(BF)
-                stage[pl.ds(base, CHUNK), which] = got.reshape(CHUNK, SLOTS, WIDTH)
+        return ones, scaled
+
+    def pack(g, half, mats, srcs, cols, out, arrived):
+        take = slice(half * CHUNK * SLOTS, (half + 1) * CHUNK * SLOTS)
+        base = g * EXPERTS + half * CHUNK
+        for which, (mat, src) in enumerate(zip(mats, srcs)):
+            got = dot(mat[:, take], src[:, cols], ((0,), (0,))).astype(BF)
+            got = got.reshape(CHUNK, SLOTS, got.shape[1])
+            out[pl.ds(base, CHUNK), which] = got
             if half == 0:
-                local_dispatch(g).start()
-            for o in range(half * CHUNK, (half + 1) * CHUNK):
-                if o:
-                    dispatch(g, o).start()
-
-    pack(0, x_ref, dy_ref)
+                arrived[base, which] = got[0]
+
+    def send(g, lo, hi):
+        for o in range(max(lo, 1), hi):
+            dispatch(g, o).start()
+
+    own_masks = masks(0)
+    for half in range(EXPERTS // CHUNK):
+        pack(0, half, own_masks, (x_ref, dy_ref), pl.ds(MAIN, REST), stage_b, rows_b)
+        if half == 0:
+            across(0).start()
+        for o in range(max(half * CHUNK, 1), (half + 1) * CHUNK):
+            dispatch_rest(o).start()
+    pack(0, 0, own_masks, (x_ref, dy_ref), pl.ds(0, MAIN), stage, rows)
+    send(0, 0, CHUNK)
+    pack(0, 1, own_masks, (x_ref, dy_ref), pl.ds(0, MAIN), stage, rows)
+    send(0, CHUNK, EARLY)
+
+    def pass_on(o, _):
+        dispatch_rest(o).wait_recv()
+        across(o).start()
+        return 0
+
+    lax.fori_loop(1, EXPERTS, pass_on, 0)
+    for c in z_copies:
+        c.wait_recv()
+    mate_masks = masks(1)
+    for half in range(EXPERTS // CHUNK):
+        pack(1, half, mate_masks, (pair.at[0], pair.at[1]), pl.ds(0, MAIN), stage, rows)
+        send(1, half * CHUNK, (half + 1) * CHUNK)
+    send(0, EARLY, EXPERTS)
     for c in w_copies:
         c.wait()
 
     def work(i, _):
-        g = i // (EXPERTS // CHUNK)
-        first = (i % (EXPERTS // CHUNK)) * CHUNK
-
-        @pl.when(i == 1)
-        def _():
-            for c in z_copies:
-                c.wait_recv()
-            pack(1, pair.at[0], pair.at[1])
-
-        @pl.when(first == 0)
-        def _():
-            local_dispatch(g).wait()
+        g = (i + 1) // 2 % 2
+        first = i // 2 * CHUNK
 
         def arrive(j, _):
             o = first + j
@@ -163,16 +196,22 @@
             def _():
                 dispatch(g, o).wait_recv()
 
+            @pl.when(g == 1)
+            def _():
+                across(o).wait_recv()
+
             return 0
 
         lax.fori_loop(0, CHUNK, arrive, 0)
-        f = pl.multiple_of(i * CHUNK, CHUNK)
-        r = pl.multiple_of(i * CHUNK * SLOTS, CHUNK * SLOTS)
+        f = pl.multiple_of(g * EXPERTS + first, CHUNK)
+        r = pl.multiple_of(f * SLOTS, CHUNK * SLOTS)
         n = CHUNK * SLOTS
-        x = rows[pl.ds(f, CHUNK), 0].reshape(n, WIDTH)
-        dyp = rows[pl.ds(f, CHUNK), 1].reshape(n, WIDTH)
-        ab = dot(x, wgu[...], ((1,), (0,)))
-        q = dot(dyp, wdn[...], ((1,), (1,)))
+        x = rows[pl.ds(f, CHUNK), 0].reshape(n, MAIN)
+        dyp = rows[pl.ds(f, CHUNK), 1].reshape(n, MAIN)
+        x_b = rows_b[pl.ds(f, CHUNK), 0].reshape(n, REST)
+        dyp_b = rows_b[pl.ds(f, CHUNK), 1].reshape(n, REST)
+        ab = dot(x, wgu[pl.ds(0, MAIN), :], ((1,), (0,))) + dot(x_b, wgu[pl.ds(MAIN, REST), :], ((1,), (0,)))
+        q = dot(dyp, wdn[:, pl.ds(0, MAIN)], ((1,), (1,))) + dot(dyp_b, wdn[:, pl.ds(MAIN, REST)], ((1,), (1,)))
         a, b = ab[:, :HALF], ab[:, HALF:]
         sig = jax.nn.sigmoid(a)
         act = a * sig
@@ -209,26 +248,6 @@
 
     lax.fori_loop(0, 2 * EXPERTS // CHUNK, work, 0)
 
-    n_rows = 2 * EXPERTS * SLOTS
-    tile = 256
-
-    def grads(t, _):
-        cols = pl.ds(pl.multiple_of(t * tile, tile), tile)
-        xt = rows[:, 0, :, cols].reshape(n_rows, tile)
-        ggu[cols, :] = dot(xt, dab[...], ((0,), (0,))).astype(BF)
-        dyt = rows[:, 1, :, cols].reshape(n_rows, tile)
-        gdn[:, cols] = dot(hid[...], dyt, ((0,), (0,))).astype(BF)
-        return 0
-
-    lax.fori_loop(0, WIDTH // tile, grads, 0)
-    o_copies = [
-        pltpu.make_async_copy(ggu.at[:, pl.ds(0, HALF)], gg_ref, o_sem.at[0]),
-        pltpu.make_async_copy(ggu.at[:, pl.ds(HALF, HALF)], gu_ref, o_sem.at[1]),
-        pltpu.make_async_copy(gdn, gd_ref, o_sem.at[2]),
-    ]
-    for c in o_copies:
-        c.start()
-
     def join(g):
         local_giveback(g).wait()
 
@@ -247,16 +266,42 @@
         parts = [dot(hits[k].astype(BF), tail, ((1,), (0,))) for k in range(2)]
         return [v[:, 0:1] + v[:, 1:2] for v in parts]
 
-    own = join(0)
     other = join(1)
     rfin_out[...] = jnp.where(lane == 0, other[0], jnp.where(lane == 1, other[1], 0.0))
     final(2).start()
 
+    n_rows = 2 * EXPERTS * SLOTS
+    tile = 256
+
+    def grads(held, start):
+        def one(t, _):
+            cols = pl.ds(pl.multiple_of(t * tile, tile), tile)
+            to = pl.ds(pl.multiple_of(start + t * tile, tile), tile)
+            xt = held[:, 0, :, cols].reshape(n_rows, tile)
+            ggu[to, :] = dot(xt, dab[...], ((0,), (0,))).astype(BF)
+            dyt = held[:, 1, :, cols].reshape(n_rows, tile)
+            gdn[:, to] = dot(hid[...], dyt, ((0,), (0,))).astype(BF)
+            return 0
+
+        lax.fori_loop(0, held.shape[3] // tile, one, 0)
+
+    grads(rows, 0)
+    grads(rows_b, MAIN)
+    o_copies = [
+        pltpu.make_async_copy(ggu.at[:, pl.ds(0, HALF)], gg_ref, o_sem.at[0]),
+        pltpu.make_async_copy(ggu.at[:, pl.ds(HALF, HALF)], gu_ref, o_sem.at[1]),
+        pltpu.make_async_copy(gdn, gd_ref, o_sem.at[2]),
+    ]
+    for c in o_copies:
+        c.start()
+
+    own = join(0)
     final(2).wait_recv()
     there = rfin_in[...]
-    total = [(own[k] + there[:, k : k + 1]) / probs[:, k : k + 1] for k in range(2)]
-    pairs = jnp.where(lane == 0, total[0], jnp.where(lane == 1, total[1], 0.0))
-    rg_ref[...] = pairs[:, :2].astype(BF)
+    total = [(own[k] + there[:, k : k + 1]) / probs[k] for k in range(2)]
+    lines = [jnp.sum(jnp.where(diagonal, v, 0.0), axis=0, keepdims=True) for v in total]
+    which = lax.broadcasted_iota(jnp.int32, (2, TOK), 0)
+    rg_ref[...] = jnp.where(which == 0, lines[0], lines[1]).astype(BF)
     final(0).wait_recv()
     final(1).wait_recv()
     summed = fin_in[0].astype(F32) + fin_in[1].astype(F32)
@@ -271,8 +316,11 @@
         for g in range(2):
             dispatch(g, o).wait_send()
             giveback(g, o).wait_send()
+        dispatch_rest(o).wait_send()
+        across(o).wait_send()
         return 0
 
+    across(0).wait_send()
     lax.fori_loop(1, EXPERTS, left, 0)
     for c in o_copies:
         c.wait()
@@ -287,7 +335,7 @@
         kernel,
         out_shape=(
             jax.ShapeDtypeStruct((TOK, WIDTH), BF),
-            jax.ShapeDtypeStruct((TOK, 2), BF),
+            jax.ShapeDtypeStruct((2, TOK), BF),
             jax.ShapeDtypeStruct((WIDTH, HALF), BF),
             jax.ShapeDtypeStruct((WIDTH, HALF), BF),
             jax.ShapeDtypeStruct((HALF, WIDTH), BF),
@@ -297,10 +345,12 @@
         scratch_shapes=[
             pltpu.VMEM((WIDTH, 2 * HALF), BF),
             pltpu.VMEM((HALF, WIDTH), BF),
-            pltpu.VMEM((2, TOK, WIDTH), BF),
+            pltpu.VMEM((2, TOK, MAIN), BF),
             pltpu.VMEM((2, TOK, TOK), BF),
-            pltpu.VMEM((blocks, 2, SLOTS, WIDTH), BF),
-            pltpu.VMEM((blocks, 2, SLOTS, WIDTH), BF),
+            pltpu.VMEM((blocks, 2, SLOTS, MAIN), BF),
+            pltpu.VMEM((EXPERTS, 2, SLOTS, REST), BF),
+            pltpu.VMEM((blocks, 2, SLOTS, MAIN), BF),
+            pltpu.VMEM((blocks, 2, SLOTS, REST), BF),
             pltpu.VMEM((n_rows, 2 * HALF), BF),
             pltpu.VMEM((n_rows, HALF), BF),
             pltpu.VMEM((blocks, SLOTS, WIDTH + TAIL), BF),
@@ -316,6 +366,10 @@
             pltpu.SemaphoreType.DMA((3,)),
             pltpu.SemaphoreType.DMA((blocks,)),
             pltpu.SemaphoreType.DMA((blocks,)),
+            pltpu.SemaphoreType.DMA((EXPERTS,)),
+            pltpu.SemaphoreType.DMA((EXPERTS,)),
+            pltpu.SemaphoreType.DMA((EXPERTS,)),
+            pltpu.SemaphoreType.DMA((EXPERTS,)),
             pltpu.SemaphoreType.DMA((blocks,)),
             pltpu.SemaphoreType.DMA((blocks,)),
             pltpu.SemaphoreType.DMA((3,)),
@@ -325,8 +379,9 @@
         ],
         compiler_params=pltpu.CompilerParams(has_side_effects=True, vmem_limit_bytes=58 << 20),
         name="expert_backward",
-    )(tokens[0], routes[0], probs[0], cotangent[0], w_gate[0], w_up[0], w_down[0])
-    return tuple(o[None] for o in out)
+    )(tokens[0], routes[0].T, probs[0].T, cotangent[0], w_gate[0], w_up[0], w_down[0])
+    upstream, route_grad, g_gate, g_up, g_down = out
+    return upstream[None], route_grad.T[None], g_gate[None], g_up[None], g_down[None]
 
 
 def solution(mesh):

time: 258 us -> 217 us (0.84); the launches traced: 258 us -> 213 us
  Pallas kernels: 245 us -> 203 us
  local copies, waits for them, and re-layouts: 12 us -> 8.93 us
    pallas_call x1, Pallas kernels: 245 us -> 203 us  [body(): pl.pallas_call(kernel, out_shape=(jax.ShapeDtypeStruct((TOK, WIDTH), BF),...]
    unnamed x11 -> x9, local copies, waits for them, and re-layouts: 12 us -> 8.93 us
where the time goes in v2:
time: 217 us; the launch traced here: 213 us
  Pallas kernels  203 us (94%)
  local copies, waits for them, and re-layouts  8.93 us (4%)
    pallas_call x1, Pallas kernels, body(): pl.pallas_call(kernel, out_shape=(jax.ShapeDtypeStruct((TOK, WIDTH), BF),...  203 us
    unnamed x9, local copies, waits for them, and re-layouts  8.93 us

profile of v2, /device:TPU:27, one launch (start us, length us, event | category | flops | bytes accessed | tf_op | source)
XLA Modules:
  0.0 212.6 jit_solution(18189966260667380939)
XLA Ops:
  0.6 203.1 %expert_backward.1 = (bf16[128,2048]{1,0:T(8,128)(2,1)}, bf16[2,128]{1,0:T(2,128)(2,1)}, bf16[2048,384]{1,0:T(8,128)(2,1)}, bf16[2048,384]{1,0:T(8,128)(2,1)}, bf16[384,2048]{1,0:T(8,128)(2,1)}) custom-call(bf16[128,2048]{1,0:T(8,128)(2,1)} %bitcast.24, s32[2,128]{1,0:T(2,128)} %bitcast.27, bf16[2,128]{1,0:T(2,128)(2,1)} %bitcast.28, ...), custom_call_target="tpu_custom_call" | custom-call | tf_op jit(solution)/shard_map/expert_backward/pallas_call | solution.py:334
  203.7 1.9 copy.17
  205.6 1.1 copy.18
  206.7 0.0 copy-start.1
  206.7 2.8 %copy.19 = bf16[1,2048,384]{2,1,0:T(8,128)(2,1)} copy(bf16[1,2048,384]{2,1,0:T(8,128)(2,1)} %bitcast.20) | data formatting | bytes 3145728
  209.5 0.0 copy-done.1
  209.5 0.0 copy-start
  209.5 1.1 copy.20
  210.7 0.8 copy-done
  211.5 1.1 copy.21
Async XLA Ops:
  206.7 2.8 %copy-start.1 = (bf16[2048,384]{1,0:T(8,128)(2,1)S(1)}, bf16[2048,384]{1,0:T(8,128)(2,1)}, u32[]{:S(2)}) copy-start(bf16[2048,384]{1,0:T(8,128)(2,1)} %get-tuple-element.13) | copy-start | bytes 4718596
  209.5 2.0 copy-start

commit v3 on v2

--- a/solution.py
+++ b/solution.py
@@ -15,7 +15,7 @@
 HALF = 384
 TAIL = 128
 CHUNK = 8
-REST = 512
+REST = 768
 MAIN = WIDTH - REST
 EARLY = 12
 MESH = pl.DeviceIdType.MESH
@@ -100,6 +100,14 @@
         return pltpu.make_async_remote_copy(
             src_ref=src, dst_ref=dst, send_sem=f_send.at[i], recv_sem=f_recv.at[i],
             device_id=to, device_id_type=MESH)
+
+    following = (sec + 1) % n_sec
+    gate = pltpu.get_barrier_semaphore()
+    others = [{"expert": ahead(o)} for o in range(1, EXPERTS)] + [{"expert": mate}]
+    others += [{"section": s, "expert": u} for s in (prev, following) for u in (unit, mate)]
+    for other in others:
+        pl.semaphore_signal(gate, inc=1, device_id=other, device_id_type=MESH)
+    pl.semaphore_wait(gate, len(others))
 
     z_copies[0].start()
     z_copies[1].start()
@@ -323,6 +331,20 @@
     across(0).wait_send()
     lax.fori_loop(1, EXPERTS, left, 0)
     for c in o_copies:
+        c.wait()
+
+
+def hand_on(*refs):
+    n = len(refs) // 3
+    sems = refs[-1]
+    copies_in = [pltpu.make_async_copy(refs[i], refs[2 * n + i], sems.at[0, i]) for i in range(n)]
+    copies_out = [pltpu.make_async_copy(refs[2 * n + i], refs[n + i], sems.at[1, i]) for i in range(n)]
+    for c in copies_in:
+        c.start()
+    for arrived, c in zip(copies_in, copies_out):
+        arrived.wait()
+        c.start()
+    for c in copies_out:
         c.wait()
 
 
@@ -377,10 +399,18 @@
             pltpu.SemaphoreType.DMA((2,)),
             pltpu.SemaphoreType.DMA((3,)),
         ],
-        compiler_params=pltpu.CompilerParams(has_side_effects=True, vmem_limit_bytes=58 << 20),
+        compiler_params=pltpu.CompilerParams(collective_id=0, has_side_effects=True, vmem_limit_bytes=58 << 20),
         name="expert_backward",
     )(tokens[0], routes[0].T, probs[0].T, cotangent[0], w_gate[0], w_up[0], w_down[0])
-    upstream, route_grad, g_gate, g_up, g_down = out
+    upstream, route_grad, g_gate, g_up, g_down = pl.pallas_call(
+        hand_on,
+        out_shape=tuple(jax.ShapeDtypeStruct(o.shape, o.dtype) for o in out),
+        in_specs=[hbm] * len(out),
+        out_specs=(hbm,) * len(out),
+        scratch_shapes=[pltpu.VMEM(o.shape, o.dtype) for o in out] + [pltpu.SemaphoreType.DMA((2, len(out)))],
+        compiler_params=pltpu.CompilerParams(vmem_limit_bytes=58 << 20),
+        name="hand_on",
+    )(*out)
     return upstream[None], route_grad.T[None], g_gate[None], g_up[None], g_down[None]
 
 

time: 217 us -> 185 us (0.85)
  the two profiles are of different devices: /device:TPU:27 before, /device:TPU:42 now
where the time goes in v3:
time: 185 us
  Pallas kernels  185 us (100%)
    pallas_call x1, Pallas kernels, body(): pl.pallas_call(kernel, out_shape=(jax.ShapeDtypeStruct((TOK, WIDTH), BF),...  180 us
    pallas_call x1, Pallas kernels, body(): pl.pallas_call(hand_on, out_shape=tuple((jax.ShapeDtypeStruct(o.shape, o....  4.35 us

profile of v3, /device:TPU:42, one launch (start us, length us, event | category | flops | bytes accessed | tf_op | source)
XLA Modules:
  0.0 185.2 jit_solution(3489666156248563726)
XLA Ops:
  0.6 180.2 %expert_backward.1 = (bf16[128,2048]{1,0:T(8,128)(2,1)}, bf16[2,128]{1,0:T(2,128)(2,1)}, bf16[2048,384]{1,0:T(8,128)(2,1)}, bf16[2048,384]{1,0:T(8,128)(2,1)}, bf16[384,2048]{1,0:T(8,128)(2,1)}) custom-call(bf16[128,2048]{1,0:T(8,128)(2,1)} %bitcast.21, s32[2,128]{1,0:T(2,128)} %bitcast.23, bf16[2,128]{1,0:T(2,128)(2,1)} %bitcast.24, ...), custom_call_target="tpu_custom_call" | custom-call | tf_op jit(solution)/shard_map/expert_backward/pallas_call | solution.py:356
  180.8 4.4 %hand_on.1 = (bf16[128,2048]{1,0:T(8,128)(2,1)}, bf16[2,128]{1,0:T(2,128)(2,1)}, bf16[2048,384]{1,0:T(8,128)(2,1)}, bf16[2048,384]{1,0:T(8,128)(2,1)}, bf16[384,2048]{1,0:T(8,128)(2,1)}) custom-call(bf16[128,2048]{1,0:T(8,128)(2,1)} %get-tuple-element.15.refs_0_, bf16[2,128]{1,0:T(2,128)(2,1)} %get-tuple-element.16.refs_1_, ...), custom_call_target="tpu_custom_call" | custom-call | tf_op jit(solution)/shard_map/hand_on/pallas_call | solution.py:405

commit v4 on v3

--- a/solution.py
+++ b/solution.py
@@ -17,7 +17,10 @@
 CHUNK = 8
 REST = 768
 MAIN = WIDTH - REST
-EARLY = 12
+FAR = 1024
+NEAR = WIDTH - FAR
+PART = NEAR + TAIL
+EARLY = 16
 MESH = pl.DeviceIdType.MESH
 
 
@@ -28,9 +31,9 @@
 def kernel(
     x_ref, routes_ref, probs_ref, dy_ref, wg_ref, wu_ref, wd_ref,
     up_ref, rg_ref, gg_ref, gu_ref, gd_ref,
-    wgu, wdn, pair, metas, stage, stage_b, rows, rows_b, dab, hid, ret_out, ret_in, ggu, gdn,
+    wgu, wdn, pair, metas, stage, stage_b, rows, rows_b, dab, hid, ret_out, ret_in, summand, ggu, gdn,
     fin_out, fin_in, rfin_out, rfin_in,
-    w_sem, z_send, z_recv, d_send, d_recv, b_send, b_recv, c_send, c_recv, r_send, r_recv, f_send, f_recv, l_sem, o_sem,
+    w_sem, z_send, z_recv, d_send, d_recv, b_send, b_recv, c_send, c_recv, r_send, r_recv, f_send, f_recv, s_send, s_recv, l_sem, o_sem,
 ):
     sec = lax.axis_index("section")
     unit = lax.axis_index("expert")
@@ -90,6 +93,17 @@
             src_ref=ret_out.at[f], dst_ref=ret_in.at[f], send_sem=r_send.at[f], recv_sem=r_recv.at[f],
             device_id={"expert": behind(o)}, device_id_type=MESH)
 
+    def giveback_part(o):
+        f = EXPERTS + o
+        cols = pl.ds(0, PART)
+        return pltpu.make_async_remote_copy(
+            src_ref=ret_out.at[f, :, cols], dst_ref=ret_in.at[f, :, cols], send_sem=r_send.at[f],
+            recv_sem=r_recv.at[f], device_id={"expert": behind(o)}, device_id_type=MESH)
+
+    summand_copy = pltpu.make_async_remote_copy(
+        src_ref=ret_out.at[pl.ds(EXPERTS + CHUNK, CHUNK), :, pl.ds(PART, FAR)], dst_ref=summand,
+        send_sem=s_send, recv_sem=s_recv, device_id={"expert": mate}, device_id_type=MESH)
+
     def local_giveback(g):
         f = g * EXPERTS
         return pltpu.make_async_copy(ret_out.at[f], ret_in.at[f], l_sem.at[g])
@@ -107,10 +121,6 @@
     others += [{"section": s, "expert": u} for s in (prev, following) for u in (unit, mate)]
     for other in others:
         pl.semaphore_signal(gate, inc=1, device_id=other, device_id_type=MESH)
-    pl.semaphore_wait(gate, len(others))
-
-    z_copies[0].start()
-    z_copies[1].start()
     for c in w_copies:
         c.start()
 
@@ -137,7 +147,6 @@
         meta = jnp.where(lane == 2 * k + 1, place, meta)
         meta = jnp.where(lane == 4 + k, probs[k], meta)
     metas[0] = meta.astype(BF)
-    z_copies[2].start()
 
     def picks(g):
         m = metas[g].astype(F32)
@@ -168,11 +177,14 @@
     own_masks = masks(0)
     for half in range(EXPERTS // CHUNK):
         pack(0, half, own_masks, (x_ref, dy_ref), pl.ds(MAIN, REST), stage_b, rows_b)
-        if half == 0:
-            across(0).start()
-        for o in range(max(half * CHUNK, 1), (half + 1) * CHUNK):
-            dispatch_rest(o).start()
     pack(0, 0, own_masks, (x_ref, dy_ref), pl.ds(0, MAIN), stage, rows)
+
+    pl.semaphore_wait(gate, len(others))
+    for c in z_copies:
+        c.start()
+    across(0).start()
+    for o in range(1, EXPERTS):
+        dispatch_rest(o).start()
     send(0, 0, CHUNK)
     pack(0, 1, own_masks, (x_ref, dy_ref), pl.ds(0, MAIN), stage, rows)
     send(0, CHUNK, EARLY)
@@ -231,12 +243,28 @@
         dab[pl.ds(r, n), pl.ds(0, HALF)] = d_gate
         dab[pl.ds(r, n), pl.ds(HALF, HALF)] = d_up
         both = dab[pl.ds(r, n), :]
-        back = dot(both, wgu[...], ((1,), (1,))).astype(BF)
-        ret_out[pl.ds(f, CHUNK), :, pl.ds(0, WIDTH)] = back.reshape(CHUNK, SLOTS, WIDTH)
+        back = dot(both, wgu[...], ((1,), (1,)))
+        ret_out[pl.ds(f, CHUNK), :, pl.ds(0, NEAR)] = back[:, :NEAR].astype(BF).reshape(CHUNK, SLOTS, NEAR)
+        far = back[:, NEAR:]
+
+        @pl.when(i < 3)
+        def _():
+            ret_out[pl.ds(f, CHUNK), :, pl.ds(PART, FAR)] = far.astype(BF).reshape(CHUNK, SLOTS, FAR)
+
+        @pl.when(i == 2)
+        def _():
+            summand_copy.start()
+
+        @pl.when(i == 3)
+        def _():
+            summand_copy.wait_recv()
+            both_halves = far + summand[...].reshape(n, FAR).astype(F32)
+            ret_out[pl.ds(f, CHUNK), :, pl.ds(PART, FAR)] = both_halves.astype(BF).reshape(CHUNK, SLOTS, FAR)
+
         high = part.astype(BF).astype(F32)
         at = lax.broadcasted_iota(jnp.int32, (n, TAIL), 1)
         tail = jnp.where(at == 0, high, jnp.where(at == 1, part - high, 0.0)).astype(BF)
-        ret_out[pl.ds(f, CHUNK), :, pl.ds(WIDTH, TAIL)] = tail.reshape(CHUNK, SLOTS, TAIL)
+        ret_out[pl.ds(f, CHUNK), :, pl.ds(NEAR, TAIL)] = tail.reshape(CHUNK, SLOTS, TAIL)
 
         @pl.when(first == 0)
         def _():
@@ -245,10 +273,14 @@
         def leave(j, _):
             o = first + j
 
-            @pl.when(o > 0)
+            @pl.when((o > 0) & (i != 2))
             def _():
                 giveback(g, o).start()
 
+            @pl.when(i == 2)
+            def _():
+                giveback_part(o).start()
+
             return 0
 
         lax.fori_loop(0, CHUNK, leave, 0)
@@ -258,19 +290,28 @@
 
     def join(g):
         local_giveback(g).wait()
+
+        whole = EXPERTS if g == 0 else CHUNK
 
         def arrive(o, _):
             giveback(g, o).wait_recv()
             return 0
 
-        lax.fori_loop(1, EXPERTS, arrive, 0)
+        def arrive_part(o, _):
+            giveback_part(o).wait_recv()
+            return 0
+
+        lax.fori_loop(1, whole, arrive, 0)
+        lax.fori_loop(whole, EXPERTS, arrive_part, 0)
         hits, _ = picks(g)
         got = ret_in.at[pl.ds(g * EXPERTS, EXPERTS)]
         mine = (hits[0] | hits[1]).astype(BF)
-        dx = dot(mine, got[:, :, pl.ds(0, WIDTH)].reshape(EXPERTS * SLOTS, WIDTH), ((1,), (0,)))
-        fin_out[g] = dx.astype(BF)
+        near = got[:, :, pl.ds(0, NEAR)].reshape(EXPERTS * SLOTS, NEAR)
+        fin_out[g, :, pl.ds(0, NEAR)] = dot(mine, near, ((1,), (0,))).astype(BF)
+        far = got[pl.ds(0, whole), :, pl.ds(PART, FAR)].reshape(whole * SLOTS, FAR)
+        fin_out[g, :, pl.ds(NEAR, FAR)] = dot(mine[:, : whole * SLOTS], far, ((1,), (0,))).astype(BF)
         final(g).start()
-        tail = got[:, :, pl.ds(WIDTH, TAIL)].reshape(EXPERTS * SLOTS, TAIL)
+        tail = got[:, :, pl.ds(NEAR, TAIL)].reshape(EXPERTS * SLOTS, TAIL)
         parts = [dot(hits[k].astype(BF), tail, ((1,), (0,))) for k in range(2)]
         return [v[:, 0:1] + v[:, 1:2] for v in parts]
 
@@ -320,15 +361,26 @@
     for i in range(3):
         final(i).wait_send()
 
+    summand_copy.wait_send()
+    across(0).wait_send()
+
     def left(o, _):
         for g in range(2):
             dispatch(g, o).wait_send()
-            giveback(g, o).wait_send()
         dispatch_rest(o).wait_send()
         across(o).wait_send()
+        giveback(0, o).wait_send()
+
+        @pl.when(o < CHUNK)
+        def _():
+            giveback(1, o).wait_send()
+
+        @pl.when(o >= CHUNK)
+        def _():
+            giveback_part(o).wait_send()
+
         return 0
 
-    across(0).wait_send()
     lax.fori_loop(1, EXPERTS, left, 0)
     for c in o_copies:
         c.wait()
@@ -377,6 +429,7 @@
             pltpu.VMEM((n_rows, HALF), BF),
             pltpu.VMEM((blocks, SLOTS, WIDTH + TAIL), BF),
             pltpu.VMEM((blocks, SLOTS, WIDTH + TAIL), BF),
+            pltpu.VMEM((CHUNK, SLOTS, FAR), BF),
             pltpu.VMEM((WIDTH, 2 * HALF), BF),
             pltpu.VMEM((HALF, WIDTH), BF),
             pltpu.VMEM((2, TOK, WIDTH), BF),
@@ -396,6 +449,8 @@
             pltpu.SemaphoreType.DMA((blocks,)),
             pltpu.SemaphoreType.DMA((3,)),
             pltpu.SemaphoreType.DMA((3,)),
+            pltpu.SemaphoreType.DMA,
+            pltpu.SemaphoreType.DMA,
             pltpu.SemaphoreType.DMA((2,)),
             pltpu.SemaphoreType.DMA((3,)),
         ],

time: 185 us -> 182 us (0.984)
  the two profiles are of different devices: /device:TPU:42 before, /device:TPU:97 now
where the time goes in v4:
time: 182 us
  Pallas kernels  182 us (100%)
    pallas_call x1, Pallas kernels, body(): pl.pallas_call(kernel, out_shape=(jax.ShapeDtypeStruct((TOK, WIDTH), BF),...  177 us
    pallas_call x1, Pallas kernels, body(): pl.pallas_call(hand_on, out_shape=tuple((jax.ShapeDtypeStruct(o.shape, o....  4.35 us

profile of v4, /device:TPU:97, one launch (start us, length us, event | category | flops | bytes accessed | tf_op | source)
XLA Modules:
  0.0 182.4 jit_solution(6350438956484409584)
XLA Ops:
  0.6 177.4 %expert_backward.1 = (bf16[128,2048]{1,0:T(8,128)(2,1)}, bf16[2,128]{1,0:T(2,128)(2,1)}, bf16[2048,384]{1,0:T(8,128)(2,1)}, bf16[2048,384]{1,0:T(8,128)(2,1)}, bf16[384,2048]{1,0:T(8,128)(2,1)}) custom-call(bf16[128,2048]{1,0:T(8,128)(2,1)} %bitcast.21, s32[2,128]{1,0:T(2,128)} %bitcast.23, bf16[2,128]{1,0:T(2,128)(2,1)} %bitcast.24, ...), custom_call_target="tpu_custom_call" | custom-call | tf_op jit(solution)/shard_map/expert_backward/pallas_call | solution.py:408
  178.0 4.4 %hand_on.1 = (bf16[128,2048]{1,0:T(8,128)(2,1)}, bf16[2,128]{1,0:T(2,128)(2,1)}, bf16[2048,384]{1,0:T(8,128)(2,1)}, bf16[2048,384]{1,0:T(8,128)(2,1)}, bf16[384,2048]{1,0:T(8,128)(2,1)}) custom-call(bf16[128,2048]{1,0:T(8,128)(2,1)} %get-tuple-element.15.refs_0_, bf16[2,128]{1,0:T(2,128)(2,1)} %get-tuple-element.16.refs_1_, ...), custom_call_target="tpu_custom_call" | custom-call | tf_op jit(solution)/shard_map/hand_on/pallas_call | solution.py:460

commit v5 on v4

--- a/solution.py
+++ b/solution.py
@@ -17,7 +17,7 @@
 CHUNK = 8
 REST = 768
 MAIN = WIDTH - REST
-FAR = 1024
+FAR = 640
 NEAR = WIDTH - FAR
 PART = NEAR + TAIL
 EARLY = 16

time: 182 us -> 180 us (0.989)
  the two profiles are of different devices: /device:TPU:97 before, /device:TPU:12 now
where the time goes in v5:
time: 180 us; the launch traced here: 179 us
  Pallas kernels  179 us (99%)
    pallas_call x1, Pallas kernels, body(): pl.pallas_call(kernel, out_shape=(jax.ShapeDtypeStruct((TOK, WIDTH), BF),...  174 us
    pallas_call x1, Pallas kernels, body(): pl.pallas_call(hand_on, out_shape=tuple((jax.ShapeDtypeStruct(o.shape, o....  4.35 us

profile of v5, /device:TPU:12, one launch (start us, length us, event | category | flops | bytes accessed | tf_op | source)
XLA Modules:
  0.0 179.5 jit_solution(7107626133151735368)
XLA Ops:
  0.6 174.5 %expert_backward.1 = (bf16[128,2048]{1,0:T(8,128)(2,1)}, bf16[2,128]{1,0:T(2,128)(2,1)}, bf16[2048,384]{1,0:T(8,128)(2,1)}, bf16[2048,384]{1,0:T(8,128)(2,1)}, bf16[384,2048]{1,0:T(8,128)(2,1)}) custom-call(bf16[128,2048]{1,0:T(8,128)(2,1)} %bitcast.21, s32[2,128]{1,0:T(2,128)} %bitcast.23, bf16[2,128]{1,0:T(2,128)(2,1)} %bitcast.24, ...), custom_call_target="tpu_custom_call" | custom-call | tf_op jit(solution)/shard_map/expert_backward/pallas_call | solution.py:408
  175.1 4.4 %hand_on.1 = (bf16[128,2048]{1,0:T(8,128)(2,1)}, bf16[2,128]{1,0:T(2,128)(2,1)}, bf16[2048,384]{1,0:T(8,128)(2,1)}, bf16[2048,384]{1,0:T(8,128)(2,1)}, bf16[384,2048]{1,0:T(8,128)(2,1)}) custom-call(bf16[128,2048]{1,0:T(8,128)(2,1)} %get-tuple-element.15.refs_0_, bf16[2,128]{1,0:T(2,128)(2,1)} %get-tuple-element.16.refs_1_, ...), custom_call_target="tpu_custom_call" | custom-call | tf_op jit(solution)/shard_map/hand_on/pallas_call | solution.py:460
